TPU v7x, 32 devices: a whole 2x2x4 slice. The times are simulated.
32 devices in a mesh: groups: 2 (over x), bus: 16 (over z, y, core).
Axes of the slice: x: 2, y: 2, z: 4, core: 2. Of those that a mesh axis runs over, the one named last changes fastest.
Arguments:
- generation: float32 [512, 32], P('bus', 'groups'), parts along dimension 1, may hold values from 0 to 1
- charging: float32 [32, 512], P('groups', 'bus'), parts along dimension 0, may hold values from -1.5 to 1.5
- flow_dual: float32 [4096, 32], P('bus', 'groups'), parts along dimension 1, may hold values from -3 to 3
- energy_dual: float32 [32, 512], P('groups', 'bus'), parts along dimension 0, may hold values from -1.6 to 1.6
- shift_factors: float32 [4096, 16384], P(None, 'bus'), may hold values from -0.0625 to 0.0625
- load_units: int32 [16384, 32], P('bus', 'groups'), parts along dimension 1, may hold values from 0 to 59
- generator_bus: int32 [512], P('bus'), may hold values from 0 to 16383, as said below
- storage_bus: int32 [512], P('bus'), may hold values from 0 to 16383, as said below
- generator_cost: float32 [512], P('bus'), may hold values from 0.05 to 0.5
- generator_max: float32 [512], P('bus'), may hold values from 1 to 4
- charging_max: float32 [512], replicated, may hold values from 2 to 4
- energy_init: float32 [512], replicated, may hold values from 0.5 to 2
- energy_max: float32 [512], replicated, may hold values from 2.5 to 4
- line_max: float32 [4096], P('bus'), may hold values from 0.5 to 3
Outputs:
- generation_new: float32 [512, 32], P('bus', 'groups'), parts along dimension 1
- charging_new: float32 [32, 512], P('groups', 'bus'), parts along dimension 0
- flow_dual_new: float32 [4096, 32], P('bus', 'groups'), parts along dimension 1
- energy_dual_new: float32 [32, 512], P('groups', 'bus'), parts along dimension 0
There are 2 independent parts, one for each index of `groups`. A program takes and returns all parts, laid end to end along the dimension named above; an argument that names none is the same for every part. Nothing has to cross between parts.
Inputs may be any that keep to these rules, and one draw needn't show every extreme that they name: `generator_bus`: generator g sits at one of the buses g // 32 * 1024 to (g // 32 + 1) * 1024 - 1. `storage_bus`: storage unit k sits at one of the buses k // 32 * 1024 to (k // 32 + 1) * 1024 - 1.
All inputs are finite; a program needn't handle non-finite values.
Results may differ from a plain program's by a relative error of at most 0.00023.
Values sent between devices are 32-bit elements; how exact they have to be, the bound alone decides.
No kernel may reach another device: no remote copies, remote signals or barrier semaphores. Data moves between devices by JAX's collectives and lax.ppermute only.
A program may use at most 64 MiB of HBM per device.

v0:
```python
import jax
import jax.numpy as jnp
from jax import lax
from jax.sharding import PartitionSpec as P

ITERS = 3


primal_step = 0.5
dual_step = 0.5
energy_step = 0.05
efficiency = 0.95
interval = 0.125
load_unit = 0.05
highest = lax.Precision.HIGHEST
across_first = (((0,), (0,)), ((), ()))
across_second = (((1,), (1,)), ((), ()))
inner_pair = (((1,), (0,)), ((), ()))


def contract(left, right, dims):
    return lax.dot_general(left, right, dims, precision=highest, preferred_element_type=jnp.float32)


def reverse_cumsum(values):
    return jnp.flip(jnp.cumsum(jnp.flip(values, 0), axis=0), 0)


def clip_dual(shifted, step_size, low_bound, high_bound):
    return shifted - step_size * jnp.clip(shifted / step_size, low_bound, high_bound)


def on_device(
    generation,
    charging,
    flow_dual,
    energy_dual,
    shift_factors,
    load_units,
    generator_bus,
    storage_bus,
    generator_cost,
    generator_max,
    charging_max,
    energy_init,
    energy_max,
    line_max,
):
    bus_local = shift_factors.shape[1]
    stor_local = storage_bus.shape[0]
    own_index = lax.axis_index("bus")
    bus_ids = lax.broadcasted_iota(jnp.int32, (bus_local, 1), 0) + own_index * bus_local
    gen_onehot = (generator_bus[None, :] == bus_ids).astype(jnp.float32)
    stor_onehot = (storage_bus[None, :] == bus_ids).astype(jnp.float32)
    demand = load_units.astype(jnp.float32) * load_unit
    unit_cost = generator_cost[:, None]
    ceiling = generator_max[:, None]
    first_slot = own_index * stor_local
    charge_limit = lax.dynamic_slice_in_dim(charging_max, first_slot, stor_local)[None, :]
    start_energy = lax.dynamic_slice_in_dim(energy_init, first_slot, stor_local)[None, :]
    energy_limit = lax.dynamic_slice_in_dim(energy_max, first_slot, stor_local)[None, :]
    for iteration in range(ITERS):
        prices = contract(
            shift_factors, lax.all_gather(flow_dual, "bus", axis=0, tiled=True), across_first
        )
        gen_step = jnp.clip(
            generation - primal_step * (unit_cost + contract(gen_onehot, prices, across_first)),
            0.0,
            ceiling,
        )
        gen_bar = 2.0 * gen_step - generation
        stor_prices = contract(prices, stor_onehot, across_first)
        gradient = efficiency * interval * reverse_cumsum(energy_dual) - stor_prices
        charge_step = jnp.clip(charging - primal_step * gradient, -charge_limit, charge_limit)
        bar_bus = 2.0 * charge_step - charging
        energy = start_energy + efficiency * interval * jnp.cumsum(bar_bus, axis=0)
        energy_dual = clip_dual(energy_dual + energy_step * energy, energy_step, 0.0, energy_limit)
        charging = charge_step
        injected = (
            contract(gen_onehot, gen_bar, inner_pair)
            - contract(stor_onehot, bar_bus, across_second)
            - demand
        )
        line_flows = lax.psum_scatter(
            contract(shift_factors, injected, inner_pair), "bus", scatter_dimension=0, tiled=True
        )
        flow_dual = clip_dual(
            flow_dual + dual_step * line_flows, dual_step, -line_max[:, None], line_max[:, None]
        )
        generation = gen_step
    return (generation, charging, flow_dual, energy_dual)


def solution(mesh):
    placed = (
        P("bus", "groups"),
        P("groups", "bus"),
        P("bus", "groups"),
        P("groups", "bus"),
        P(None, "bus"),
        P("bus", "groups"),
        P("bus"),
        P("bus"),
        P("bus"),
        P("bus"),
        P(),
        P(),
        P(),
        P("bus"),
    )
    return jax.shard_map(
        on_device,
        mesh=mesh,
        in_specs=placed,
        out_specs=(P("bus", "groups"), P("groups", "bus"), P("bus", "groups"), P("groups", "bus")),
        check_vma=False,
    )
```

profile of v0, /device:TPU:0, one launch (start us, length us, event | category | flops | bytes accessed | tf_op | source)
XLA Modules:
  0.0 335.1 jit_solution(3252353573156793211)
XLA Ops:
  7.2 0.0 copy-start.11
  7.2 0.0 copy-start.8
  7.2 0.0 copy-start.7
  7.2 0.0 copy-start.10
  7.2 0.0 reduce-scatter.4.cloned.1.call-start
  7.3 0.7 rev.19
  8.0 24.1 %all_gather.9 = f32[4096,16]{0,1:T(8,128)S(1)} all-gather(f32[256,16]{0,1:T(8,128)} %param.16), channel_id=1, replica_groups=mesh['groups'=2,'bus'=16] {'bus'}, dimensions={0}, use_global_device_ids=true | all-gather | bytes 278528 | tf_op jit(solution)/shard_map/all_gather | solution.py:64
  32.1 0.9 fusion.168
  33.0 12.9 %fusion.169 = f32[1024,16]{0,1:T(8,128)S(1)} fusion(f32[4096,1024]{1,0:T(8,128)} %param.18, f32[4096,16]{0,1:T(8,128)S(1)} %all_gather.9), kind=kOutput, calls=%fused_computation.111 | convolution fusion | flops 805306368 | bytes 17104896 | tf_op jit(solution)/shard_map/dot_general | solution.py:22
  46.0 0.0 copy-done.11
  46.0 0.0 copy-done.8
  46.0 0.4 multiply_subtract_fusion.8
  46.4 0.5 fusion.8
  46.9 0.0 copy-done.10
  46.9 0.4 fusion.54
  47.3 0.5 fusion.27
  47.8 0.0 copy-done
  47.8 14.9 %convolution_bitcast_fusion.2 = f32[4096,16]{0,1:T(8,128)} fusion(f32[1024,16]{0,1:T(8,128)S(1)} %fusion.27, f32[4096,1024]{1,0:T(8,128)S(1)} %copy-done), kind=kOutput, calls=%fused_computation.2 | convolution fusion | flops 805306368 | bytes 17104896 | tf_op jit(solution)/shard_map/dot_general | solution.py:22
  62.6 0.0 reduce-scatter.4.cloned.1.call-update
  62.7 0.0 reduce-scatter.6.cloned.1.call-start
  62.7 0.8 dynamic_slice.10
  63.5 0.8 dynamic_slice.11
  64.3 51.5 %reduce-scatter.4.cloned.1.call-done = f32[256,16]{0,1:T(8,128)} async-done(((f32[4096,16]{0,1:T(8,128)}), f32[256,16]{0,1:T(8,128)}) %reduce-scatter.4.cloned.1.call-update) | async-done | bytes 16400 | tf_op jit(solution)/shard_map/reduce_scatter | solution.py:84
  115.8 0.7 multiply_subtract_fusion.2
  116.5 20.2 %all_gather.10 = f32[4096,16]{0,1:T(8,128)S(1)} all-gather(f32[256,16]{0,1:T(8,128)S(1)} %multiply_subtract_fusion.2), channel_id=1, replica_groups=mesh['groups'=2,'bus'=16] {'bus'}, dimensions={0}, use_global_device_ids=true | all-gather | bytes 278528 | tf_op jit(solution)/shard_map/all_gather | solution.py:64
  136.7 11.6 %fusion.170 = f32[16,1024]{1,0:T(8,128)S(1)} fusion(f32[4096,16]{0,1:T(8,128)S(1)} %all_gather.10, f32[4096,1024]{1,0:T(8,128)} %param.18), kind=kOutput, calls=%fused_computation.112 | convolution fusion | flops 805306368 | bytes 17104896 | tf_op jit(solution)/shard_map/dot_general | solution.py:22
  148.3 0.4 fusion.69
  148.6 0.4 multiply_subtract_fusion.6
  149.0 0.5 fusion.4
  149.5 0.5 fusion.33
  150.0 17.8 %convolution_bitcast_fusion.1 = f32[4096,16]{0,1:T(8,128)} fusion(f32[1024,16]{0,1:T(8,128)S(1)} %fusion.33, f32[4096,1024]{1,0:T(8,128)} %param.18), kind=kOutput, calls=%fused_computation.1 | convolution fusion | flops 805306368 | bytes 17104896 | tf_op jit(solution)/shard_map/dot_general | solution.py:22
  167.8 0.0 reduce-scatter.6.cloned.1.call-update
  167.8 0.0 reduce-scatter.8.cloned.1.call-start
  167.9 53.0 %reduce-scatter.6.cloned.1.call-done = f32[256,16]{0,1:T(8,128)} async-done(((f32[4096,16]{0,1:T(8,128)}), f32[256,16]{0,1:T(8,128)}) %reduce-scatter.6.cloned.1.call-update) | async-done | bytes 16400 | tf_op jit(solution)/shard_map/reduce_scatter | solution.py:84
  220.9 0.7 multiply_subtract_fusion.1
  221.6 20.2 %all_gather.11 = f32[4096,16]{0,1:T(8,128)S(1)} all-gather(f32[256,16]{0,1:T(8,128)S(1)} %multiply_subtract_fusion.1), channel_id=1, replica_groups=mesh['groups'=2,'bus'=16] {'bus'}, dimensions={0}, use_global_device_ids=true | all-gather | bytes 278528 | tf_op jit(solution)/shard_map/all_gather | solution.py:64
  241.8 11.8 %fusion.171 = f32[16,1024]{1,0:T(8,128)S(1)} fusion(f32[4096,16]{0,1:T(8,128)S(1)} %all_gather.11, f32[4096,1024]{1,0:T(8,128)} %param.18), kind=kOutput, calls=%fused_computation.113 | convolution fusion | flops 805306368 | bytes 17104896 | tf_op jit(solution)/shard_map/dot_general | solution.py:22
  253.6 0.4 fusion.84
  254.0 0.0 copy-start.6
  254.0 1.0 multiply_subtract_fusion.4
  255.0 0.4 fusion
  255.4 0.5 fusion.39
  255.9 17.8 %convolution_bitcast_fusion = f32[4096,16]{0,1:T(8,128)} fusion(f32[1024,16]{0,1:T(8,128)S(1)} %fusion.39, f32[4096,1024]{1,0:T(8,128)} %param.18), kind=kOutput, calls=%fused_computation | convolution fusion | flops 805306368 | bytes 17104896 | tf_op jit(solution)/shard_map/dot_general | solution.py:22
  273.7 0.0 reduce-scatter.8.cloned.1.call-update
  273.8 0.6 multiply_subtract_fusion.3
  274.4 52.5 %reduce-scatter.8.cloned.1.call-done = f32[256,16]{0,1:T(8,128)} async-done(((f32[4096,16]{0,1:T(8,128)}), f32[256,16]{0,1:T(8,128)}) %reduce-scatter.8.cloned.1.call-update) | async-done | bytes 16400 | tf_op jit(solution)/shard_map/reduce_scatter | solution.py:84
  326.8 1.3 multiply_subtract_fusion
  328.2 0.0 copy-done.6
  (29 shorter events, 0.3 us)
Async XLA Ops:
  7.2 38.8 %copy-start.11 = (s32[32]{0:T(128)S(1)}, s32[32]{0:T(128)}, u32[]{:S(2)}) copy-start(s32[32]{0:T(128)} %param.21) | copy-start | bytes 388
  7.2 38.8 %copy-start.8 = (f32[16,32]{1,0:T(8,128)S(1)}, f32[16,32]{1,0:T(8,128)}, u32[]{:S(2)}) copy-start(f32[16,32]{1,0:T(8,128)} %param.15) | copy-start | bytes 6148
  7.2 39.7 %copy-start.7 = (s32[32]{0:T(128)S(1)}, s32[32]{0:T(128)}, u32[]{:S(2)}) copy-start(s32[32]{0:T(128)} %param.20) | copy-start | bytes 388
  7.2 39.7 %copy-start.10 = (f32[32]{0:T(128)S(1)}, f32[32]{0:T(128)}, u32[]{:S(2)}) copy-start(f32[32]{0:T(128)} %param.23) | copy-start | bytes 388
  7.2 39.7 %copy-start.9 = (f32[32]{0:T(128)S(1)}, f32[32]{0:T(128)}, u32[]{:S(2)}) copy-start(f32[32]{0:T(128)} %param.22) | copy-start | bytes 388
  7.2 39.7 %copy-start.5 = (f32[32,16]{0,1:T(8,128)S(1)}, f32[32,16]{0,1:T(8,128)}, u32[]{:S(2)}) copy-start(f32[32,16]{0,1:T(8,128)} %param.14) | copy-start | bytes 6148
  7.2 40.1 %copy-start.1 = (s32[1024,16]{0,1:T(8,128)S(1)}, s32[1024,16]{0,1:T(8,128)}, u32[]{:S(2)}) copy-start(s32[1024,16]{0,1:T(8,128)} %param.19) | copy-start | bytes 196612
  7.2 108.6 %reduce-scatter.4.cloned.1.call-start = ((), (), s32[]{:S(2)}) async-start(), calls=%async_computation.3 | async-start | bytes 278528 | tf_op jit(solution)/shard_map/reduce_scatter | solution.py:84
  32.1 15.6 %copy-start = (f32[4096,1024]{1,0:T(8,128)S(1)}, f32[4096,1024]{1,0:T(8,128)}, u32[]{:S(2)}) copy-start(f32[4096,1024]{1,0:T(8,128)} %param.18) | copy-start | bytes 50331652
  33.0 31.2 %copy-start.4 = (f32[256]{0:T(256)S(1)}, f32[256]{0:T(256)}, u32[]{:S(2)}) copy-start(f32[256]{0:T(256)} %param.27) | copy-start | bytes 3076
  33.0 31.2 %copy-start.3 = (f32[16,32]{1,0:T(8,128)S(1)}, f32[16,32]{1,0:T(8,128)}, u32[]{:S(2)}) copy-start(f32[16,32]{1,0:T(8,128)} %param.17) | copy-start | bytes 6148
  33.0 82.8 %copy-start.2 = (f32[256,16]{0,1:T(8,128)S(1)}, f32[256,16]{0,1:T(8,128)}, u32[]{:S(2)}) copy-start(f32[256,16]{0,1:T(8,128)} %param.16) | copy-start | bytes 49156
  62.7 158.3 %reduce-scatter.6.cloned.1.call-start = ((), (), s32[]{:S(2)}) async-start(), calls=%async_computation.4 | async-start | bytes 278528 | tf_op jit(solution)/shard_map/reduce_scatter | solution.py:84
  167.8 159.0 %reduce-scatter.8.cloned.1.call-start = ((), (), s32[]{:S(2)}) async-start(), calls=%async_computation.5 | async-start | bytes 278528 | tf_op jit(solution)/shard_map/reduce_scatter | solution.py:84
  254.0 74.2 %copy-start.6 = (f32[32,16]{0,1:T(8,128)}, f32[32,16]{0,1:T(8,128)S(1)}, u32[]{:S(2)}) copy-start(f32[32,16]{0,1:T(8,128)S(1)} %fusion.84) | copy-start | bytes 6148
Sparse Core Ops, SparseCore 0:
  62.8 52.9 reduce-scatter.3
  167.9 52.9 reduce-scatter.5
  273.8 52.9 reduce-scatter.7
where the time goes:
time: 340 us; the launch traced here: 335 us
  waiting for transfers between devices  157 us (46%)
  matrix products  92.4 us (27%)
  blocking collectives  64.4 us (19%)
  between operations  14.4 us (4%)
  other arithmetic  4.55 us (1%)
    reduce_scatter x3, waiting for transfers between devices, on_device(): lax.psum_scatter(contract(shift_factors, injected, inner_pair), 'bus', sc...  157 us
    dot_general x18, matrix products, contract(): lax.dot_general(left, right, dims, precision=highest, preferred_element_t...  92.4 us
    all_gather x3, blocking collectives, on_device(): lax.all_gather(flow_dual, 'bus', axis=0, tiled=True)  64.4 us
  transfers between devices with their start and end apart: 3, of which 3 were waited for; matrix products, arithmetic and copies ran while one was open for 1% of the time, Pallas kernels for 0%

commit v1 on v0

v1 whole, which is shorter than its diff:
```python
import functools

import jax
import jax.numpy as jnp
from jax import lax
from jax.experimental import pallas as pl
from jax.experimental.pallas import tpu as pltpu
from jax.sharding import PartitionSpec as P

ITERS = 3


primal_step = 0.5
dual_step = 0.5
energy_step = 0.05
efficiency = 0.95
interval = 0.125
load_unit = 0.05
rows_by_cols = (((1,), (0,)), ((), ()))
rows_by_rows = (((1,), (1,)), ((), ()))


def split_halves(values):
    high = values.astype(jnp.bfloat16)
    low = (values - high.astype(jnp.float32)).astype(jnp.bfloat16)
    return high, low


def matmul(left, right, dims):
    return lax.dot_general(left, right, dims, preferred_element_type=jnp.float32)


def clip_dual(shifted, step_size, low_bound, high_bound):
    return shifted - step_size * jnp.clip(shifted / step_size, low_bound, high_bound)


def running_sum(values, reverse):
    count = values.shape[0]
    shift = 1
    while shift < count:
        zeros = jnp.zeros((shift, values.shape[1]), values.dtype)
        if reverse:
            moved = jnp.concatenate([values[shift:], zeros], axis=0)
        else:
            moved = jnp.concatenate([zeros, values[:-shift]], axis=0)
        values = values + moved
        shift *= 2
    return values


def scan_kernel(order, factors, weights, columns, base_flow, *, units):
    high, low = split_halves(factors[...])
    w = weights[...]
    found = matmul(high, w, rows_by_cols) + matmul(low, w, rows_by_cols)
    turned = found.T
    top, bottom = split_halves(turned[:units])
    columns[:units, :] = top
    columns[units:, :] = bottom
    base_flow[...] = load_unit * turned[units:]


def scan_factors(order, factors, weights, units, tile):
    lines, buses = factors.shape
    width = weights.shape[1]
    horizon = width - units
    return pl.pallas_call(
        functools.partial(scan_kernel, units=units),
        grid_spec=pltpu.PrefetchScalarGridSpec(
            num_scalar_prefetch=1,
            grid=(lines // tile,),
            in_specs=[
                pl.BlockSpec((tile, buses), lambda i, order: (i, 0)),
                pl.BlockSpec((buses, width), lambda i, order: (0, 0)),
            ],
            out_specs=[
                pl.BlockSpec((2 * units, tile), lambda i, order: (0, order[i])),
                pl.BlockSpec((horizon, tile), lambda i, order: (0, order[i])),
            ],
        ),
        out_shape=[
            jax.ShapeDtypeStruct((2 * units, lines), jnp.bfloat16),
            jax.ShapeDtypeStruct((horizon, lines), jnp.float32),
        ],
        name="scan_factors",
    )(order, factors, weights)


def unit_kernel(
    columns, base_flow, dual, generation, charging, energy_dual, params,
    new_generation, new_charging, new_energy_dual, flows,
):
    horizon, gens = generation.shape
    units = columns.shape[0] // 2
    dual_high, dual_low = split_halves(dual[...])
    cols = columns[...]
    parts = matmul(jnp.concatenate([dual_high, dual_low], axis=0), cols, rows_by_rows)
    prices = parts[:horizon, :units] + parts[:horizon, units:] + parts[horizon:, :units]
    old = generation[...]
    cost = params[0:1, :]
    ceiling = params[1:2, :]
    charge_limit = params[2:3, :]
    start_energy = params[3:4, :]
    energy_limit = params[4:5, :]
    gen_step = jnp.clip(old - primal_step * (cost + prices[:, :gens]), 0.0, ceiling)
    gen_bar = 2.0 * gen_step - old
    new_generation[...] = gen_step
    duals = energy_dual[...]
    held = charging[...]
    gradient = efficiency * interval * running_sum(duals, True) - prices[:, gens:]
    charge_step = jnp.clip(held - primal_step * gradient, -charge_limit, charge_limit)
    charge_bar = 2.0 * charge_step - held
    new_charging[...] = charge_step
    energy = start_energy + efficiency * interval * running_sum(charge_bar, False)
    new_energy_dual[...] = clip_dual(duals + energy_step * energy, energy_step, 0.0, energy_limit)
    bars_high, bars_low = split_halves(jnp.concatenate([gen_bar, -charge_bar], axis=1))
    bars = jnp.concatenate(
        [
            jnp.concatenate([bars_high, bars_high], axis=1),
            jnp.concatenate([bars_low, jnp.zeros_like(bars_low)], axis=1),
        ],
        axis=0,
    )
    both = matmul(bars, cols, rows_by_cols)
    flows[...] = both[:horizon] + both[horizon:] - base_flow[...]


def step_units(columns, base_flow, dual, generation, charging, energy_dual, params):
    like = lambda a: jax.ShapeDtypeStruct(a.shape, jnp.float32)
    return pl.pallas_call(
        unit_kernel,
        out_shape=[like(generation), like(charging), like(energy_dual), like(base_flow)],
        name="step_units",
    )(columns, base_flow, dual, generation, charging, energy_dual, params)


def exchange(values, bit, count):
    return lax.ppermute(values, "bus", [(i, i ^ bit) for i in range(count)])


def on_device(
    generation,
    charging,
    flow_dual,
    energy_dual,
    shift_factors,
    load_units,
    generator_bus,
    storage_bus,
    generator_cost,
    generator_max,
    charging_max,
    energy_init,
    energy_max,
    line_max,
    *,
    count,
):
    lines, buses = shift_factors.shape
    own_lines, horizon = flow_dual.shape
    stor_local = storage_bus.shape[0]
    own = lax.axis_index("bus")
    near_bits = [bit for bit in (1, 2) if bit < count]
    far_bits = [bit for bit in (1 << k for k in range(2, 30)) if bit < count]
    near = 1 << len(near_bits)
    far = count // near
    own_near = own % near
    own_far = own // near
    block = jnp.arange(count, dtype=jnp.int32)
    relative = (block % near) ^ own_near
    turned = jnp.zeros_like(relative)
    for k in range(len(near_bits)):
        turned = turned + ((relative >> k) & 1) * (near >> (k + 1))
    order = turned * far + block // near

    unit_ids = jnp.concatenate([generator_bus, storage_bus])[None, :] - own * buses
    picks = lax.broadcasted_iota(jnp.int32, (buses, 1), 0) == unit_ids
    weights = jnp.concatenate(
        [picks.astype(jnp.bfloat16), load_units.astype(jnp.bfloat16)], axis=1
    )
    units = unit_ids.shape[1]
    if own_lines % 128 == 0:
        columns, base_flow = scan_factors(order, shift_factors, weights, units, own_lines)
    else:
        tile = min(lines, 512)
        plain = jnp.arange(lines // tile, dtype=jnp.int32)
        place = jnp.zeros_like(order).at[order].set(block)
        columns, base_flow = [
            jnp.take(found.reshape(found.shape[0], count, own_lines), place, axis=1).reshape(
                found.shape
            )
            for found in scan_factors(plain, shift_factors, weights, units, tile)
        ]

    first_slot = own * stor_local
    mine = lambda a: lax.dynamic_slice_in_dim(a, first_slot, stor_local)
    params = jnp.stack(
        [generator_cost, generator_max, mine(charging_max), mine(energy_init), mine(energy_max)]
    )

    def sum_far(values):
        for bit in far_bits:
            values = values + exchange(values, bit, count)
        return values

    def gather_near(values):
        for bit in reversed(near_bits):
            values = jnp.concatenate([values, exchange(values, bit, count)], axis=1)
        return values

    def scatter_near(values):
        for bit in near_bits:
            half = values.shape[1] // 2
            values = values[:, :half] + exchange(values[:, half:], bit, count)
        return values

    start = jnp.concatenate([flow_dual.T, line_max[None, :]], axis=0)
    placed = lax.dynamic_update_slice(
        jnp.zeros((horizon + 1, far * own_lines), jnp.float32), start, (0, own_far * own_lines)
    )
    placed = sum_far(placed)
    dual = placed[:horizon]
    limit = placed[horizon:]
    gen_state = generation.T
    for iteration in range(ITERS):
        gen_state, charging, energy_dual, flows = step_units(
            columns, base_flow, gather_near(dual), gen_state, charging, energy_dual, params
        )
        dual = clip_dual(
            dual + dual_step * sum_far(scatter_near(flows)), dual_step, -limit, limit
        )
    own_dual = lax.dynamic_slice_in_dim(dual, own_far * own_lines, own_lines, axis=1)
    return (gen_state.T, charging, own_dual.T, energy_dual)


def solution(mesh):
    placed = (
        P("bus", "groups"),
        P("groups", "bus"),
        P("bus", "groups"),
        P("groups", "bus"),
        P(None, "bus"),
        P("bus", "groups"),
        P("bus"),
        P("bus"),
        P("bus"),
        P("bus"),
        P(),
        P(),
        P(),
        P("bus"),
    )
    return jax.shard_map(
        functools.partial(on_device, count=mesh.shape["bus"]),
        mesh=mesh,
        in_specs=placed,
        out_specs=(P("bus", "groups"), P("groups", "bus"), P("bus", "groups"), P("groups", "bus")),
        check_vma=False,
    )
```

time: 340 us -> 116 us (0.34); the launches traced: 335 us -> 115 us
  waiting for transfers between devices: 157 us -> 59.2 us
  matrix products: 92.4 us -> 0 us
  blocking collectives: 64.4 us -> 0 us
  Pallas kernels: 0 us -> 26.6 us
  between operations: 14.4 us -> 0.89 us
  starting transfers between devices: 0.12 us -> 13.6 us
  other arithmetic: 4.55 us -> 10.3 us
    reduce_scatter x3 -> x0, waiting for transfers between devices: 157 us -> none  [on_device(): lax.psum_scatter(contract(shift_factors, injected, inner_pair), 'bus', sc...]
    dot_general x18 -> x0, matrix products: 92.4 us -> none  [contract(): lax.dot_general(left, right, dims, precision=highest, preferred_element_t...]
    all_gather x3 -> x0, blocking collectives: 64.4 us -> none  [on_device(): lax.all_gather(flow_dual, 'bus', axis=0, tiled=True)]
    ppermute x0 -> x20, waiting for transfers between devices: none -> 59.2 us  [exchange(): return lax.ppermute(values, 'bus', [(i, i ^ bit) for i in range(count)])]
    pallas_call x0 -> x4, Pallas kernels: none -> 26.6 us  [the longest x1 16.5 us: scan_factors(): pl.pallas_call(functools.partial(scan_kernel, units=units), grid_spec=plt...]
    ppermute x0 -> x20, starting transfers between devices: none -> 13.6 us  [exchange(): return lax.ppermute(values, 'bus', [(i, i ^ bit) for i in range(count)])]
    add x1 -> x12, other arithmetic: 0.01 us -> 4.11 us  [the longest x6 2.81 us: scatter_near(): values = values[:, :half] + exchange(values[:, half:], bit, count)]
  transfers between devices with their start and end apart: 3 -> 20, of which waited for: 3 -> 19; matrix products, arithmetic and copies ran while one was open for 1% -> 4% of each run, Pallas kernels for 0% -> 14%
where the time goes in v1:
time: 116 us; the launch traced here: 115 us
  waiting for transfers between devices  59.2 us (51%)
  Pallas kernels  26.6 us (23%)
  starting transfers between devices  13.6 us (12%)
  other arithmetic  10.3 us (9%)
  local copies, waits for them, and re-layouts  4.57 us (4%)
    ppermute x20, waiting for transfers between devices, exchange(): return lax.ppermute(values, 'bus', [(i, i ^ bit) for i in range(count)])  59.2 us
    pallas_call x1, Pallas kernels, scan_factors(): pl.pallas_call(functools.partial(scan_kernel, units=units), grid_spec=plt...  16.5 us
    ppermute x20, starting transfers between devices, exchange(): return lax.ppermute(values, 'bus', [(i, i ^ bit) for i in range(count)])  13.6 us
    pallas_call x3, Pallas kernels, step_units(): pl.pallas_call(unit_kernel, out_shape=[like(generation), like(charging),...  10.1 us
    add x6, other arithmetic, scatter_near(): values = values[:, :half] + exchange(values[:, half:], bit, count)  2.81 us
    slice x6, local copies, waits for them, and re-layouts, scatter_near(): values = values[:, :half] + exchange(values[:, half:], bit, count)  2.76 us
  transfers between devices with their start and end apart: 20, of which 19 were waited for; matrix products, arithmetic and copies ran while one was open for 4% of the time, Pallas kernels for 14%

profile of v1, /device:TPU:0, one launch (start us, length us, event | category | flops | bytes accessed | tf_op | source)
XLA Modules:
  0.0 115.2 jit_solution(5587223865894928929)
XLA Ops:
  0.7 0.7 fusion.1
  1.5 3.1 %collective-permute-start = (f32[17,1024]{1,0:T(8,128)S(1)}, f32[17,1024]{1,0:T(8,128)S(1)}, u32[]{:S(2)}, u32[]{:S(2)}) collective-permute-start(f32[17,1024]{1,0:T(8,128)S(1)} %fusion.1), channel_id=1, source_target_pairs={{0,4},{1,5},{2,6},{3,7},{4,0},{5,1},{6,2},{7,3},{8,12},{9,13},{10,... | collective-permute-start | bytes 208904 | tf_op jit(solution)/shard_map/ppermute | solution.py:137
  4.5 0.7 add_subtract_fusion
  5.3 0.8 convert_element_type.7
  6.4 0.9 collective-permute-done
  7.3 0.7 add_dynamic-update-slice_fusion
  8.0 2.8 %collective-permute-start.1 = (f32[17,1024]{1,0:T(8,128)S(1)}, f32[17,1024]{1,0:T(8,128)S(1)}, u32[]{:S(2)}, u32[]{:S(2)}) collective-permute-start(f32[17,1024]{1,0:T(8,128)S(1)} %add_dynamic-update-slice_fusion), channel_id=1, source_target_pairs={{0,8},{1,9},{2,10},{3,11},{4,12},{5,13},{6,14},{7,15},{8,0},{9,1},... | collective-permute-start | bytes 208904 | tf_op jit(solution)/shard_map/ppermute | solution.py:137
  10.9 0.9 pad_maximum_fusion.weights
  11.7 3.3 %collective-permute-done.1 = f32[17,1024]{1,0:T(8,128)S(1)} collective-permute-done((f32[17,1024]{1,0:T(8,128)S(1)}, f32[17,1024]{1,0:T(8,128)S(1)}, u32[]{:S(2)}, u32[]{:S(2)}) %collective-permute-start.1) | collective-permute-done | bytes 69664 | tf_op jit(solution)/shard_map/ppermute | solution.py:137
  15.4 0.5 fusion.2.order
  15.9 3.4 %collective-permute-done.2 = f32[16,1024]{1,0:T(8,128)S(1)} collective-permute-done((f32[16,1024]{1,0:T(8,128)S(1)}, f32[16,1024]{1,0:T(8,128)S(1)}, u32[]{:S(2)}, u32[]{:S(2)}) %collective-permute-start.2) | collective-permute-done | bytes 65568 | tf_op jit(solution)/shard_map/ppermute | solution.py:137
  19.5 16.5 %scan_factors.1 = (bf16[128,4096]{1,0:T(8,128)(2,1)}, f32[16,4096]{1,0:T(8,128)}) custom-call(s32[16]{0:T(128)} %fusion.2.order, f32[4096,1024]{1,0:T(8,128)} %factors.1, bf16[1024,80]{1,0:T(8,128)(2,1)} %pad_maximum_fusion.weights), custom_call_target="tpu_custom_call" | custom-call | tf_op jit(solution)/shard_map/scan_factors/pallas_call | solution.py:66
  36.1 0.8 dynamic-slice_bitcast_fusion
  36.9 0.6 stack.23.params
  37.5 0.7 pad_maximum_fusion.1.dual
  38.2 3.4 %step_units.3 = (f32[16,32]{1,0:T(8,128)}, f32[16,32]{1,0:T(8,128)}, f32[16,32]{1,0:T(8,128)}, f32[16,4096]{1,0:T(8,128)}) custom-call(bf16[128,4096]{1,0:T(8,128)(2,1)} %get-tuple-element.18.columns, f32[16,4096]{1,0:T(8,128)} %get-tuple-element.19.base_flow, f32[16,4096]{1,0:T(8,128)} %pad_maximum_fusion.1.dual, f32[16,32]{1,0:T(8,128)} %bitcast.24, ...), custom_call_target="tpu_custom_call" | custom-call | tf_op jit(solution)/shard_map/step_units/pallas_call | solution.py:129
  41.6 0.9 slice.44
  42.5 0.6 collective-permute-start.4
  43.1 1.0 collective-permute-done.4
  44.0 0.9 slice_add_fusion.2
  45.4 4.0 %collective-permute-done.5 = f32[16,1024]{1,0:T(8,128)S(1)} collective-permute-done((f32[16,1024]{1,0:T(8,128)S(1)}, f32[16,1024]{1,0:T(8,128)S(1)}, u32[]{:S(2)}, u32[]{:S(2)}) %collective-permute-start.5) | collective-permute-done | bytes 65568 | tf_op jit(solution)/shard_map/ppermute | solution.py:137
  49.4 0.6 collective-permute-start.6
  50.0 3.7 %collective-permute-done.6 = f32[16,1024]{1,0:T(8,128)S(1)} collective-permute-done((f32[16,1024]{1,0:T(8,128)S(1)}, f32[16,1024]{1,0:T(8,128)S(1)}, u32[]{:S(2)}, u32[]{:S(2)}) %collective-permute-start.6) | collective-permute-done | bytes 65568 | tf_op jit(solution)/shard_map/ppermute | solution.py:137
  53.8 2.0 %collective-permute-start.7 = (f32[16,1024]{1,0:T(8,128)S(1)}, f32[16,1024]{1,0:T(8,128)S(1)}, u32[]{:S(2)}, u32[]{:S(2)}) collective-permute-start(f32[16,1024]{1,0:T(8,128)S(1)} %add.89), channel_id=1, source_target_pairs={{0,8},{1,9},{2,10},{3,11},{4,12},{5,13},{6,14},{7,15},{8,0},{9,1},... | collective-permute-start | bytes 196616 | tf_op jit(solution)/shard_map/ppermute | solution.py:137
  55.7 4.0 %collective-permute-done.7 = f32[16,1024]{1,0:T(8,128)S(1)} collective-permute-done((f32[16,1024]{1,0:T(8,128)S(1)}, f32[16,1024]{1,0:T(8,128)S(1)}, u32[]{:S(2)}, u32[]{:S(2)}) %collective-permute-start.7) | collective-permute-done | bytes 65568 | tf_op jit(solution)/shard_map/ppermute | solution.py:137
  59.8 4.3 %collective-permute-done.8 = f32[16,1024]{1,0:T(8,128)S(1)} collective-permute-done((f32[16,1024]{1,0:T(8,128)S(1)}, f32[16,1024]{1,0:T(8,128)S(1)}, u32[]{:S(2)}, u32[]{:S(2)}) %collective-permute-start.8) | collective-permute-done | bytes 65568 | tf_op jit(solution)/shard_map/ppermute | solution.py:137
  64.2 1.3 %collective-permute-done.9 = f32[16,2048]{1,0:T(8,128)S(1)} collective-permute-done((f32[16,2048]{1,0:T(8,128)S(1)}, f32[16,2048]{1,0:T(8,128)S(1)}, u32[]{:S(2)}, u32[]{:S(2)}) %collective-permute-start.9) | collective-permute-done | bytes 131104 | tf_op jit(solution)/shard_map/ppermute | solution.py:137
  65.5 0.7 pad_maximum_fusion.2.dual
  66.2 3.4 %step_units.4 = (f32[16,32]{1,0:T(8,128)}, f32[16,32]{1,0:T(8,128)}, f32[16,32]{1,0:T(8,128)}, f32[16,4096]{1,0:T(8,128)}) custom-call(bf16[128,4096]{1,0:T(8,128)(2,1)} %get-tuple-element.18.columns, f32[16,4096]{1,0:T(8,128)} %get-tuple-element.19.base_flow, f32[16,4096]{1,0:T(8,128)} %pad_maximum_fusion.2.dual, f32[16,32]{1,0:T(8,128)} %get-tuple-element.21.generation, ...), custom_call_target="tpu_custom_call" | custom-call | tf_op jit(solution)/shard_map/step_units/pallas_call | solution.py:129
  69.6 0.9 slice.49
  70.7 1.2 %collective-permute-done.10 = f32[16,2048]{1,0:T(8,128)S(1)} collective-permute-done((f32[16,2048]{1,0:T(8,128)S(1)}, f32[16,2048]{1,0:T(8,128)S(1)}, u32[]{:S(2)}, u32[]{:S(2)}) %collective-permute-start.10) | collective-permute-done | bytes 131104 | tf_op jit(solution)/shard_map/ppermute | solution.py:137
  71.9 0.9 slice_add_fusion.1
  72.9 4.3 %collective-permute-done.11 = f32[16,1024]{1,0:T(8,128)S(1)} collective-permute-done((f32[16,1024]{1,0:T(8,128)S(1)}, f32[16,1024]{1,0:T(8,128)S(1)}, u32[]{:S(2)}, u32[]{:S(2)}) %collective-permute-start.11) | collective-permute-done | bytes 65568 | tf_op jit(solution)/shard_map/ppermute | solution.py:137
  77.7 3.9 %collective-permute-done.12 = f32[16,1024]{1,0:T(8,128)S(1)} collective-permute-done((f32[16,1024]{1,0:T(8,128)S(1)}, f32[16,1024]{1,0:T(8,128)S(1)}, u32[]{:S(2)}, u32[]{:S(2)}) %collective-permute-start.12) | collective-permute-done | bytes 65568 | tf_op jit(solution)/shard_map/ppermute | solution.py:137
  81.5 1.4 %collective-permute-start.13 = (f32[16,1024]{1,0:T(8,128)S(1)}, f32[16,1024]{1,0:T(8,128)S(1)}, u32[]{:S(2)}, u32[]{:S(2)}) collective-permute-start(f32[16,1024]{1,0:T(8,128)S(1)} %add.94), channel_id=1, source_target_pairs={{0,8},{1,9},{2,10},{3,11},{4,12},{5,13},{6,14},{7,15},{8,0},{9,1},... | collective-permute-start | bytes 196616 | tf_op jit(solution)/shard_map/ppermute | solution.py:137
  82.9 4.4 %collective-permute-done.13 = f32[16,1024]{1,0:T(8,128)S(1)} collective-permute-done((f32[16,1024]{1,0:T(8,128)S(1)}, f32[16,1024]{1,0:T(8,128)S(1)}, u32[]{:S(2)}, u32[]{:S(2)}) %collective-permute-start.13) | collective-permute-done | bytes 65568 | tf_op jit(solution)/shard_map/ppermute | solution.py:137
  87.4 4.3 %collective-permute-done.14 = f32[16,1024]{1,0:T(8,128)S(1)} collective-permute-done((f32[16,1024]{1,0:T(8,128)S(1)}, f32[16,1024]{1,0:T(8,128)S(1)}, u32[]{:S(2)}, u32[]{:S(2)}) %collective-permute-start.14) | collective-permute-done | bytes 65568 | tf_op jit(solution)/shard_map/ppermute | solution.py:137
  91.8 1.3 %collective-permute-done.15 = f32[16,2048]{1,0:T(8,128)S(1)} collective-permute-done((f32[16,2048]{1,0:T(8,128)S(1)}, f32[16,2048]{1,0:T(8,128)S(1)}, u32[]{:S(2)}, u32[]{:S(2)}) %collective-permute-start.15) | collective-permute-done | bytes 131104 | tf_op jit(solution)/shard_map/ppermute | solution.py:137
  93.1 0.7 pad_maximum_fusion.3.dual
  93.9 3.4 %step_units.5 = (f32[16,32]{1,0:T(8,128)}, f32[16,32]{1,0:T(8,128)}, f32[16,32]{1,0:T(8,128)}, f32[16,4096]{1,0:T(8,128)}) custom-call(bf16[128,4096]{1,0:T(8,128)(2,1)} %get-tuple-element.18.columns, f32[16,4096]{1,0:T(8,128)} %get-tuple-element.19.base_flow, f32[16,4096]{1,0:T(8,128)} %pad_maximum_fusion.3.dual, f32[16,32]{1,0:T(8,128)} %get-tuple-element.25.generation, ...), custom_call_target="tpu_custom_call" | custom-call | tf_op jit(solution)/shard_map/step_units/pallas_call | solution.py:129
  97.2 0.9 slice.53
  98.4 1.2 %collective-permute-done.16 = f32[16,2048]{1,0:T(8,128)S(1)} collective-permute-done((f32[16,2048]{1,0:T(8,128)S(1)}, f32[16,2048]{1,0:T(8,128)S(1)}, u32[]{:S(2)}, u32[]{:S(2)}) %collective-permute-start.16) | collective-permute-done | bytes 131104 | tf_op jit(solution)/shard_map/ppermute | solution.py:137
  99.6 0.9 slice_add_fusion
  100.6 4.3 %collective-permute-done.17 = f32[16,1024]{1,0:T(8,128)S(1)} collective-permute-done((f32[16,1024]{1,0:T(8,128)S(1)}, f32[16,1024]{1,0:T(8,128)S(1)}, u32[]{:S(2)}, u32[]{:S(2)}) %collective-permute-start.17) | collective-permute-done | bytes 65568 | tf_op jit(solution)/shard_map/ppermute | solution.py:137
  104.9 4.3 %collective-permute-done.18 = f32[16,1024]{1,0:T(8,128)S(1)} collective-permute-done((f32[16,1024]{1,0:T(8,128)S(1)}, f32[16,1024]{1,0:T(8,128)S(1)}, u32[]{:S(2)}, u32[]{:S(2)}) %collective-permute-start.18) | collective-permute-done | bytes 65568 | tf_op jit(solution)/shard_map/ppermute | solution.py:137
  109.2 1.0 collective-permute-start.19
  110.3 4.3 %collective-permute-done.19 = f32[16,1024]{1,0:T(8,128)S(1)} collective-permute-done((f32[16,1024]{1,0:T(8,128)S(1)}, f32[16,1024]{1,0:T(8,128)S(1)}, u32[]{:S(2)}, u32[]{:S(2)}) %collective-permute-start.19) | collective-permute-done | bytes 65568 | tf_op jit(solution)/shard_map/ppermute | solution.py:137
  114.6 0.6 subtract_bitcast_fusion
  (44 shorter events, 2.9 us)
Async XLA Ops:
  0.6 18.8 %copy-start = (f32[512]{0:T(512)S(1)}, f32[512]{0:T(512)}, u32[]{:S(2)}) copy-start(f32[512]{0:T(512)} %param.24) | copy-start | bytes 6148
  0.6 36.2 %copy-start.1 = (f32[32]{0:T(128)S(1)}, f32[32]{0:T(128)}, u32[]{:S(2)}) copy-start(f32[32]{0:T(128)} %param.22) | copy-start | bytes 388
  0.7 36.2 %copy-start.2 = (f32[32]{0:T(128)S(1)}, f32[32]{0:T(128)}, u32[]{:S(2)}) copy-start(f32[32]{0:T(128)} %param.23) | copy-start | bytes 388
  1.5 5.8 %collective-permute-start = (f32[17,1024]{1,0:T(8,128)S(1)}, f32[17,1024]{1,0:T(8,128)S(1)}, u32[]{:S(2)}, u32[]{:S(2)}) collective-permute-start(f32[17,1024]{1,0:T(8,128)S(1)} %fusion.1), channel_id=1, source_target_pairs={{0,4},{1,5},{2,6},{3,7},{4,0},{5,1},{6,2},{7,3},{8,12},{9,13},{10,... | collective-permute-start | bytes 208904 | tf_op jit(solution)/shard_map/ppermute | solution.py:137
  8.0 7.0 %collective-permute-start.1 = (f32[17,1024]{1,0:T(8,128)S(1)}, f32[17,1024]{1,0:T(8,128)S(1)}, u32[]{:S(2)}, u32[]{:S(2)}) collective-permute-start(f32[17,1024]{1,0:T(8,128)S(1)} %add_dynamic-update-slice_fusion), channel_id=1, source_target_pairs={{0,8},{1,9},{2,10},{3,11},{4,12},{5,13},{6,14},{7,15},{8,0},{9,1},... | collective-permute-start | bytes 208904 | tf_op jit(solution)/shard_map/ppermute | solution.py:137
  15.0 4.3 %collective-permute-start.2 = (f32[16,1024]{1,0:T(8,128)S(1)}, f32[16,1024]{1,0:T(8,128)S(1)}, u32[]{:S(2)}, u32[]{:S(2)}) collective-permute-start(f32[16,1024]{1,0:T(8,128)S(1)} %slice.56), channel_id=1, source_target_pairs={{0,2},{1,3},{2,0},{3,1},{4,6},{5,7},{6,4},{7,5},{8,10},{9,11},{10,... | collective-permute-start | bytes 196616 | tf_op jit(solution)/shard_map/ppermute | solution.py:137
  19.4 18.1 %collective-permute-start.3 = (f32[16,2048]{1,0:T(8,128)S(1)}, f32[16,2048]{1,0:T(8,128)S(1)}, u32[]{:S(2)}, u32[]{:S(2)}) collective-permute-start(f32[16,2048]{1,0:T(8,128)S(1)} %pad_maximum_fusion.4), channel_id=1, source_target_pairs={{0,1},{1,0},{2,3},{3,2},{4,5},{5,4},{6,7},{7,6},{8,9},{9,8},{10,11... | collective-permute-start | bytes 393224 | tf_op jit(solution)/shard_map/ppermute | solution.py:137
  42.5 1.6 %collective-permute-start.4 = (f32[16,2048]{1,0:T(8,128)S(1)}, f32[16,2048]{1,0:T(8,128)S(1)}, u32[]{:S(2)}, u32[]{:S(2)}) collective-permute-start(f32[16,2048]{1,0:T(8,128)S(1)} %slice.44), channel_id=1, source_target_pairs={{0,1},{1,0},{2,3},{3,2},{4,5},{5,4},{6,7},{7,6},{8,9},{9,8},{10,11... | collective-permute-start | bytes 393224 | tf_op jit(solution)/shard_map/ppermute | solution.py:137
  45.0 4.4 %collective-permute-start.5 = (f32[16,1024]{1,0:T(8,128)S(1)}, f32[16,1024]{1,0:T(8,128)S(1)}, u32[]{:S(2)}, u32[]{:S(2)}) collective-permute-start(f32[16,1024]{1,0:T(8,128)S(1)} %slice.58), channel_id=1, source_target_pairs={{0,2},{1,3},{2,0},{3,1},{4,6},{5,7},{6,4},{7,5},{8,10},{9,11},{10,... | collective-permute-start | bytes 196616 | tf_op jit(solution)/shard_map/ppermute | solution.py:137
  49.4 4.3 %collective-permute-start.6 = (f32[16,1024]{1,0:T(8,128)S(1)}, f32[16,1024]{1,0:T(8,128)S(1)}, u32[]{:S(2)}, u32[]{:S(2)}) collective-permute-start(f32[16,1024]{1,0:T(8,128)S(1)} %slice_add_fusion.5), channel_id=1, source_target_pairs={{0,4},{1,5},{2,6},{3,7},{4,0},{5,1},{6,2},{7,3},{8,12},{9,13},{10,... | collective-permute-start | bytes 196616 | tf_op jit(solution)/shard_map/ppermute | solution.py:137
  53.8 5.9 %collective-permute-start.7 = (f32[16,1024]{1,0:T(8,128)S(1)}, f32[16,1024]{1,0:T(8,128)S(1)}, u32[]{:S(2)}, u32[]{:S(2)}) collective-permute-start(f32[16,1024]{1,0:T(8,128)S(1)} %add.89), channel_id=1, source_target_pairs={{0,8},{1,9},{2,10},{3,11},{4,12},{5,13},{6,14},{7,15},{8,0},{9,1},... | collective-permute-start | bytes 196616 | tf_op jit(solution)/shard_map/ppermute | solution.py:137
  59.7 4.3 %collective-permute-start.8 = (f32[16,1024]{1,0:T(8,128)S(1)}, f32[16,1024]{1,0:T(8,128)S(1)}, u32[]{:S(2)}, u32[]{:S(2)}) collective-permute-start(f32[16,1024]{1,0:T(8,128)S(1)} %multiply_subtract_fusion.1), channel_id=1, source_target_pairs={{0,2},{1,3},{2,0},{3,1},{4,6},{5,7},{6,4},{7,5},{8,10},{9,11},{10,... | collective-permute-start | bytes 196616 | tf_op jit(solution)/shard_map/ppermute | solution.py:137
  64.1 1.4 %collective-permute-start.9 = (f32[16,2048]{1,0:T(8,128)S(1)}, f32[16,2048]{1,0:T(8,128)S(1)}, u32[]{:S(2)}, u32[]{:S(2)}) collective-permute-start(f32[16,2048]{1,0:T(8,128)S(1)} %pad_maximum_fusion.5), channel_id=1, source_target_pairs={{0,1},{1,0},{2,3},{3,2},{4,5},{5,4},{6,7},{7,6},{8,9},{9,8},{10,11... | collective-permute-start | bytes 393224 | tf_op jit(solution)/shard_map/ppermute | solution.py:137
  70.5 1.4 %collective-permute-start.10 = (f32[16,2048]{1,0:T(8,128)S(1)}, f32[16,2048]{1,0:T(8,128)S(1)}, u32[]{:S(2)}, u32[]{:S(2)}) collective-permute-start(f32[16,2048]{1,0:T(8,128)S(1)} %slice.49), channel_id=1, source_target_pairs={{0,1},{1,0},{2,3},{3,2},{4,5},{5,4},{6,7},{7,6},{8,9},{9,8},{10,11... | collective-permute-start | bytes 393224 | tf_op jit(solution)/shard_map/ppermute | solution.py:137
  72.9 4.3 %collective-permute-start.11 = (f32[16,1024]{1,0:T(8,128)S(1)}, f32[16,1024]{1,0:T(8,128)S(1)}, u32[]{:S(2)}, u32[]{:S(2)}) collective-permute-start(f32[16,1024]{1,0:T(8,128)S(1)} %slice.61), channel_id=1, source_target_pairs={{0,2},{1,3},{2,0},{3,1},{4,6},{5,7},{6,4},{7,5},{8,10},{9,11},{10,... | collective-permute-start | bytes 196616 | tf_op jit(solution)/shard_map/ppermute | solution.py:137
  77.2 4.3 %collective-permute-start.12 = (f32[16,1024]{1,0:T(8,128)S(1)}, f32[16,1024]{1,0:T(8,128)S(1)}, u32[]{:S(2)}, u32[]{:S(2)}) collective-permute-start(f32[16,1024]{1,0:T(8,128)S(1)} %slice_add_fusion.4), channel_id=1, source_target_pairs={{0,4},{1,5},{2,6},{3,7},{4,0},{5,1},{6,2},{7,3},{8,12},{9,13},{10,... | collective-permute-start | bytes 196616 | tf_op jit(solution)/shard_map/ppermute | solution.py:137
  81.5 5.8 %collective-permute-start.13 = (f32[16,1024]{1,0:T(8,128)S(1)}, f32[16,1024]{1,0:T(8,128)S(1)}, u32[]{:S(2)}, u32[]{:S(2)}) collective-permute-start(f32[16,1024]{1,0:T(8,128)S(1)} %add.94), channel_id=1, source_target_pairs={{0,8},{1,9},{2,10},{3,11},{4,12},{5,13},{6,14},{7,15},{8,0},{9,1},... | collective-permute-start | bytes 196616 | tf_op jit(solution)/shard_map/ppermute | solution.py:137
  87.4 4.3 %collective-permute-start.14 = (f32[16,1024]{1,0:T(8,128)S(1)}, f32[16,1024]{1,0:T(8,128)S(1)}, u32[]{:S(2)}, u32[]{:S(2)}) collective-permute-start(f32[16,1024]{1,0:T(8,128)S(1)} %multiply_subtract_fusion), channel_id=1, source_target_pairs={{0,2},{1,3},{2,0},{3,1},{4,6},{5,7},{6,4},{7,5},{8,10},{9,11},{10,... | collective-permute-start | bytes 196616 | tf_op jit(solution)/shard_map/ppermute | solution.py:137
  91.7 1.4 %collective-permute-start.15 = (f32[16,2048]{1,0:T(8,128)S(1)}, f32[16,2048]{1,0:T(8,128)S(1)}, u32[]{:S(2)}, u32[]{:S(2)}) collective-permute-start(f32[16,2048]{1,0:T(8,128)S(1)} %pad_maximum_fusion.6), channel_id=1, source_target_pairs={{0,1},{1,0},{2,3},{3,2},{4,5},{5,4},{6,7},{7,6},{8,9},{9,8},{10,11... | collective-permute-start | bytes 393224 | tf_op jit(solution)/shard_map/ppermute | solution.py:137
  98.1 1.4 %collective-permute-start.16 = (f32[16,2048]{1,0:T(8,128)S(1)}, f32[16,2048]{1,0:T(8,128)S(1)}, u32[]{:S(2)}, u32[]{:S(2)}) collective-permute-start(f32[16,2048]{1,0:T(8,128)S(1)} %slice.53), channel_id=1, source_target_pairs={{0,1},{1,0},{2,3},{3,2},{4,5},{5,4},{6,7},{7,6},{8,9},{9,8},{10,11... | collective-permute-start | bytes 393224 | tf_op jit(solution)/shard_map/ppermute | solution.py:137
  100.5 4.3 %collective-permute-start.17 = (f32[16,1024]{1,0:T(8,128)S(1)}, f32[16,1024]{1,0:T(8,128)S(1)}, u32[]{:S(2)}, u32[]{:S(2)}) collective-permute-start(f32[16,1024]{1,0:T(8,128)S(1)} %slice.63), channel_id=1, source_target_pairs={{0,2},{1,3},{2,0},{3,1},{4,6},{5,7},{6,4},{7,5},{8,10},{9,11},{10,... | collective-permute-start | bytes 196616 | tf_op jit(solution)/shard_map/ppermute | solution.py:137
  104.8 4.3 %collective-permute-start.18 = (f32[16,1024]{1,0:T(8,128)S(1)}, f32[16,1024]{1,0:T(8,128)S(1)}, u32[]{:S(2)}, u32[]{:S(2)}) collective-permute-start(f32[16,1024]{1,0:T(8,128)S(1)} %slice_add_fusion.3), channel_id=1, source_target_pairs={{0,4},{1,5},{2,6},{3,7},{4,0},{5,1},{6,2},{7,3},{8,12},{9,13},{10,... | collective-permute-start | bytes 196616 | tf_op jit(solution)/shard_map/ppermute | solution.py:137
  109.2 5.4 %collective-permute-start.19 = (f32[16,1024]{1,0:T(8,128)S(1)}, f32[16,1024]{1,0:T(8,128)S(1)}, u32[]{:S(2)}, u32[]{:S(2)}) collective-permute-start(f32[16,1024]{1,0:T(8,128)S(1)} %add.99), channel_id=1, source_target_pairs={{0,8},{1,9},{2,10},{3,11},{4,12},{5,13},{6,14},{7,15},{8,0},{9,1},... | collective-permute-start | bytes 196616 | tf_op jit(solution)/shard_map/ppermute | solution.py:137
